TPU v7x, 32 devices: a whole 2x2x4 slice. The times are simulated.
32 devices in a mesh: paths: 2 (over y), tm: 16 (over z, x, core).
Axes of the slice: x: 2, y: 2, z: 4, core: 2. Of those that a mesh axis runs over, the one named last changes fastest.
Arguments:
- independent_disturbances: bfloat16 [1024, 8, 1024], P('tm', 'paths'), may hold values from -6 to 6
- starting_driver_values: float32 [8, 1024], P('paths'), may hold values from -6 to 6
- correlation_mixer: bfloat16 [1024, 1024], P('paths'), may hold values from -0.1875 to 0.1875
- log_persistence: float32 [1024], replicated, may hold values from -0.034 to 0
- regime_multiplier: float32 [1024], P('tm'), may hold values from 0.5 to 1
- payoff_per_unit_table: bfloat16 [1024, 128], replicated, may hold values from -0.1875 to 0.1875
- short_yield_coefficients: bfloat16 [1024], replicated, may hold values from -0.1875 to 0.1875
Outputs:
- values: float32 [8, 128], P('paths')
All inputs are finite; a program needn't handle non-finite values.
Results may differ from a plain program's by a relative error of at most 0.0004.
Values may be sent and summed in bfloat16 or wider, within the bound.
No kernel may reach another device: no remote copies, remote signals or barrier semaphores. Data moves between devices by JAX's collectives and lax.ppermute only.
A program may use at most 64 MiB of HBM per device.

v0:
```python
import jax
import jax.numpy as jnp
from jax import lax
from jax.sharding import PartitionSpec as P


def entering(part, axis, combine, identity):
    place = lax.axis_index(axis)
    gathered = jax.tree.map(lambda a: lax.all_gather(a, axis), part)
    state = jax.tree.map(lambda a, e: jnp.zeros_like(a) + jnp.asarray(e, a.dtype), part, identity)

    def one(turn, state):
        return combine(
            state, jax.tree.map(lambda a: lax.dynamic_index_in_dim(a, turn, 0, False), gathered)
        )

    return lax.fori_loop(0, place, one, state)


def local(
    independent_disturbances,
    starting_driver_values,
    correlation_mixer,
    log_persistence,
    regime_multiplier,
    payoff_per_unit_table,
    short_yield_coefficients,
):
    slab_days, group_paths, driver_value_history = independent_disturbances.shape
    where_now = lax.axis_index("tm")
    correlated_disturbances = jnp.einsum(
        "spf,fg->spg",
        independent_disturbances,
        lax.all_gather(correlation_mixer, "paths", axis=0, tiled=True),
        preferred_element_type=jnp.float32,
    )
    persistence_multiplier = jnp.exp(log_persistence)
    vol = jnp.sqrt(-jnp.expm1(2.0 * log_persistence))
    leading_element = jnp.where(
        where_now == 0, starting_driver_values, jnp.zeros_like(starting_driver_values)
    )

    def propagate_one_day(carry, operand_tensors):
        state, decay = carry
        random_normal_sample, regime_multiplier_today = operand_tensors
        driver_value_now = persistence_multiplier * regime_multiplier_today
        state = driver_value_now * state + vol * random_normal_sample
        decay = decay * driver_value_now
        return ((state, decay), (state, decay))

    (state, decay), (local_states, local_decays) = lax.scan(
        propagate_one_day,
        (leading_element, jnp.ones((driver_value_history,), jnp.float32)),
        (correlated_disturbances, regime_multiplier),
    )

    def chain(earlier, later):
        return (earlier[0] * later[0], later[0][None, :] * earlier[1] + later[1])

    identity = (
        jnp.ones((driver_value_history,), jnp.float32),
        jnp.zeros((group_paths, driver_value_history), jnp.float32),
    )
    carried = entering((decay, state), "tm", chain, identity)
    driver_trajectory = local_states + local_decays[:, None, :] * carried[1][None, :, :]
    scenario = driver_trajectory.astype(jnp.bfloat16)
    horizon_days = slab_days * lax.axis_size("tm")
    cash = jnp.einsum(
        "tpf,fk->tpk", scenario, payoff_per_unit_table, preferred_element_type=jnp.float32
    )
    rate = 0.03 + 0.3 * jnp.einsum(
        "tpf,f->tp", scenario, short_yield_coefficients, preferred_element_type=jnp.float32
    )
    running = jnp.cumsum(rate, axis=0)

    def added(earlier, later):
        return earlier + later

    before = entering(running[-1], "tm", added, jnp.zeros((group_paths,), jnp.float32))
    discount = jnp.exp(-(1.0 / 256.0) * (before[None, :] + running))
    partial_sum = jnp.sum(discount[:, :, None] * cash, axis=0) / horizon_days
    return lax.psum(partial_sum, "tm")


def solution(mesh):
    in_specs = (P("tm", "paths", None), P("paths", None), P("paths", None), P(), P("tm"), P(), P())
    out_specs = P("paths", None)
    return jax.shard_map(local, mesh=mesh, in_specs=in_specs, out_specs=out_specs, check_vma=False)
```

profile of v0, /device:TPU:0, one launch (start us, length us, event | category | flops | bytes accessed | tf_op | source)
XLA Modules:
  0.0 240.3 jit_solution(8618859963692799601)
XLA Ops:
  6.5 0.7 all-gather.6.cloned.1.call-update
  7.3 0.7 reshape.30
  8.0 0.7 negate_sqrt_fusion
  8.7 0.7 broadcast_select_fusion
  9.4 35.3 %all-gather.6.cloned.1.call-done = bf16[1024,1024]{1,0:T(8,128)(2,1)} async-done(((bf16[512,1024]{1,0:T(8,128)(2,1)}), bf16[1024,1024]{1,0:T(8,128)(2,1)}) %all-gather.6.cloned.1.call-update) | async-done | bytes 2097168 | tf_op jit(solution)/shard_map/all_gather | solution.py:34
  44.7 2.5 %fusion.2 = f32[64,4,1024]{2,0,1:T(8,128)S(1)} fusion(bf16[1024,1024]{1,0:T(8,128)(2,1)} %all-gather.6.cloned.1.call-done, bf16[64,4,1024]{2,1,0:T(4,128)(2,1)} %param.13), kind=kOutput, calls=%fused_computation.10 | convolution fusion | flops 536870912 | bytes 3670016 | tf_op jit(solution)/shard_map/spf,fg->spg/dot_general | solution.py:31
  47.2 95.1 %while.41 = (s32[]{:T(128)}, f32[4,1024]{1,0:T(4,128)S(1)}, f32[1024]{0:T(1024)S(1)}, f32[64,4,1024]{2,1,0:T(4,128)S(1)}, f32[64,1024]{1,0:T(8,128)S(1)}, /*inde...) while((s32[]{:T(128)}, f32[4,1024]{1,0:T(4,128)S(1)}, ...), condition=%wide.region_1.2_spmd.clone, body=%wide.region_0.1_spmd.clone.sunk | while | flops 15363 | bytes 131219 | solution.py:51
  47.3 0.7 dynamic_slice.37
  48.7 0.7 dynamic_slice.37
  50.2 0.7 dynamic_slice.37
  51.7 0.7 dynamic_slice.37
  53.2 0.7 dynamic_slice.37
  54.7 0.7 dynamic_slice.37
  56.2 0.7 dynamic_slice.37
  57.7 0.7 dynamic_slice.37
  59.1 0.7 dynamic_slice.37
  60.6 0.7 dynamic_slice.37
  62.1 0.7 dynamic_slice.37
  63.6 0.7 dynamic_slice.37
  65.1 0.7 dynamic_slice.37
  66.6 0.7 dynamic_slice.37
  68.1 0.7 dynamic_slice.37
  69.5 0.7 dynamic_slice.37
  71.0 0.7 dynamic_slice.37
  72.5 0.7 dynamic_slice.37
  74.0 0.7 dynamic_slice.37
  75.5 0.7 dynamic_slice.37
  77.0 0.7 dynamic_slice.37
  78.5 0.7 dynamic_slice.37
  79.9 0.7 dynamic_slice.37
  81.4 0.7 dynamic_slice.37
  82.9 0.7 dynamic_slice.37
  84.4 0.7 dynamic_slice.37
  85.9 0.7 dynamic_slice.37
  87.4 0.7 dynamic_slice.37
  88.9 0.7 dynamic_slice.37
  90.3 0.7 dynamic_slice.37
  91.8 0.7 dynamic_slice.37
  93.3 0.7 dynamic_slice.37
  94.8 0.7 dynamic_slice.37
  96.3 0.7 dynamic_slice.37
  97.8 0.7 dynamic_slice.37
  99.3 0.7 dynamic_slice.37
  100.7 0.7 dynamic_slice.37
  142.3 22.0 %all-gather.2 = f32[16,4,1024]{2,1,0:T(4,128)S(1)} all-gather(f32[1,4,1024]{2,1,0:T(4,128)S(1)} %bitcast.43), channel_id=3, replica_groups=mesh['paths'=2,'tm'=16] {'tm'}, dimensions={0}, use_global_device_ids=true | all-gather | bytes 278528 | tf_op jit(solution)/shard_map/all_gather | solution.py:9
  164.4 17.6 %all-gather = f32[16384]{0:T(1024)S(1)} all-gather(f32[1024]{0:T(1024)S(1)} %get-tuple-element.124), channel_id=2, replica_groups=mesh['paths'=2,'tm'=16] {'tm'}, dimensions={0}, use_global_device_ids=true | all-gather | bytes 69632 | tf_op jit(solution)/shard_map/all_gather | solution.py:9
  182.9 19.7 %all-gather.3 = f32[16,1,4]{2,1,0:T(1,128)S(1)} all-gather(f32[1,1,4]{2,1,0:T(1,128)S(1)} %slice_bitcast_fusion), channel_id=1, replica_groups=mesh['paths'=2,'tm'=16] {'tm'}, dimensions={0}, use_global_device_ids=true | all-gather | bytes 272 | tf_op jit(solution)/shard_map/all_gather | solution.py:9
  203.1 30.4 %psum.7 = f32[4,128]{1,0:T(4,128)} all-reduce(f32[4,128]{1,0:T(4,128)S(1)} %broadcast_multiply_fusion.1), channel_id=1, replica_groups=mesh['paths'=2,'tm'=16] {'tm'}, use_global_device_ids=true, to_apply=%region_8.9 | all-reduce | flops 512 | bytes 4096 | tf_op jit(solution)/shard_map/psum | solution.py:82
  (306 shorter events, 69.7 us)
Async XLA Ops:
  6.5 196.2 %copy-start = (bf16[1024,128]{1,0:T(8,128)(2,1)S(1)}, bf16[1024,128]{1,0:T(8,128)(2,1)}, u32[]{:S(2)}) copy-start(bf16[1024,128]{1,0:T(8,128)(2,1)} %param.18) | copy-start | bytes 786436
  6.5 38.2 %all-gather.6.cloned.1.call-start = ((), (), s32[]{:S(2)}) async-start(), calls=%async_computation | async-start | bytes 3145728 | tf_op jit(solution)/shard_map/all_gather | solution.py:34
  7.3 40.0 %copy-start.1 = (f32[64]{0:T(128)S(1)}, f32[64]{0:T(128)}, u32[]{:S(2)}) copy-start(f32[64]{0:T(128)} %param.17) | copy-start | bytes 772
Sparse Core Ops, SparseCore 0:
  8.9 35.8 all-gather.5
where the time goes:
time: 241 us; the launch traced here: 240 us
  blocking collectives  89.8 us (37%)
  local copies, waits for them, and re-layouts  51 us (21%)
  other arithmetic  44.2 us (18%)
  waiting for transfers between devices  36 us (15%)
  between operations  13.5 us (6%)
  matrix products  3.15 us (1%)
  loops' own time  2.71 us (1%)
    all_gather x3, blocking collectives, entering(): gathered = jax.tree.map(lambda a: lax.all_gather(a, axis), part)  59.4 us
    dynamic_slice x128, local copies, waits for them, and re-layouts, local(): lax.scan(propagate_one_day, (leading_element, jnp.ones((driver_value_hist...  43 us
    mul x64, other arithmetic, propagate_one_day(): decay = decay * driver_value_now  40.6 us
    all_gather x1, waiting for transfers between devices, local(): lax.all_gather(correlation_mixer, 'paths', axis=0, tiled=True)  35.3 us
    psum x1, blocking collectives, local(): return lax.psum(partial_sum, 'tm')  30.4 us
    dynamic_update_slice x64, local copies, waits for them, and re-layouts, local(): lax.scan(propagate_one_day, (leading_element, jnp.ones((driver_value_hist...  7.04 us
  transfers between devices with their start and end apart: 1, of which 1 were waited for; matrix products, arithmetic and copies ran while one was open for 1% of the time, Pallas kernels for 0%

commit v1 on v0

--- a/solution.py
+++ b/solution.py
@@ -79,7 +79,7 @@
     before = entering(running[-1], "tm", added, jnp.zeros((group_paths,), jnp.float32))
     discount = jnp.exp(-(1.0 / 256.0) * (before[None, :] + running))
     partial_sum = jnp.sum(discount[:, :, None] * cash, axis=0) / horizon_days
-    return lax.psum(partial_sum, "tm")
+    return jnp.sum(lax.all_gather(partial_sum, "tm"), axis=0)
 
 
 def solution(mesh):

time: 241 us -> 229 us (0.950)
  blocking collectives: 89.8 us -> 76.9 us
    psum x1 -> x0, blocking collectives: 30.4 us -> none  [local(): return lax.psum(partial_sum, 'tm')]
    all_gather x0 -> x1, blocking collectives: none -> 17.5 us  [local(): return jnp.sum(lax.all_gather(partial_sum, 'tm'), axis=0)]
where the time goes in v1:
time: 229 us; the launch traced here: 228 us
  blocking collectives  76.9 us (34%)
  local copies, waits for them, and re-layouts  51 us (22%)
  other arithmetic  44.8 us (20%)
  waiting for transfers between devices  36 us (16%)
  between operations  13.5 us (6%)
  matrix products  3.15 us (1%)
  loops' own time  2.71 us (1%)
    all_gather x3, blocking collectives, entering(): gathered = jax.tree.map(lambda a: lax.all_gather(a, axis), part)  59.4 us
    dynamic_slice x128, local copies, waits for them, and re-layouts, local(): lax.scan(propagate_one_day, (leading_element, jnp.ones((driver_value_hist...  43 us
    mul x64, other arithmetic, propagate_one_day(): decay = decay * driver_value_now  40.6 us
    all_gather x1, waiting for transfers between devices, local(): lax.all_gather(correlation_mixer, 'paths', axis=0, tiled=True)  35.3 us
    all_gather x1, blocking collectives, local(): return jnp.sum(lax.all_gather(partial_sum, 'tm'), axis=0)  17.5 us
    dynamic_update_slice x64, local copies, waits for them, and re-layouts, local(): lax.scan(propagate_one_day, (leading_element, jnp.ones((driver_value_hist...  7.04 us
  transfers between devices with their start and end apart: 1, of which 1 were waited for; matrix products, arithmetic and copies ran while one was open for 1% of the time, Pallas kernels for 0%

profile of v1, /device:TPU:0, one launch (start us, length us, event | category | flops | bytes accessed | tf_op | source)
XLA Modules:
  0.0 228.0 jit_solution(2958591011996473090)
XLA Ops:
  6.5 0.7 all-gather.8.cloned.1.call-update
  7.3 0.7 reshape.43
  8.0 0.7 negate_sqrt_fusion
  8.7 0.7 broadcast_select_fusion
  9.4 35.3 %all-gather.8.cloned.1.call-done = bf16[1024,1024]{1,0:T(8,128)(2,1)} async-done(((bf16[512,1024]{1,0:T(8,128)(2,1)}), bf16[1024,1024]{1,0:T(8,128)(2,1)}) %all-gather.8.cloned.1.call-update) | async-done | bytes 2097168 | tf_op jit(solution)/shard_map/all_gather | solution.py:34
  44.7 2.5 %fusion.2 = f32[64,4,1024]{2,0,1:T(8,128)S(1)} fusion(bf16[1024,1024]{1,0:T(8,128)(2,1)} %all-gather.8.cloned.1.call-done, bf16[64,4,1024]{2,1,0:T(4,128)(2,1)} %param.13), kind=kOutput, calls=%fused_computation.10 | convolution fusion | flops 536870912 | bytes 3670016 | tf_op jit(solution)/shard_map/spf,fg->spg/dot_general | solution.py:31
  47.2 95.1 %while.41 = (s32[]{:T(128)}, f32[4,1024]{1,0:T(4,128)S(1)}, f32[1024]{0:T(1024)S(1)}, f32[64,4,1024]{2,1,0:T(4,128)S(1)}, f32[64,1024]{1,0:T(8,128)S(1)}, /*inde...) while((s32[]{:T(128)}, f32[4,1024]{1,0:T(4,128)S(1)}, ...), condition=%wide.region_1.2_spmd.clone, body=%wide.region_0.1_spmd.clone.sunk | while | flops 15363 | bytes 131219 | solution.py:51
  47.3 0.7 dynamic_slice.37
  48.7 0.7 dynamic_slice.37
  50.2 0.7 dynamic_slice.37
  51.7 0.7 dynamic_slice.37
  53.2 0.7 dynamic_slice.37
  54.7 0.7 dynamic_slice.37
  56.2 0.7 dynamic_slice.37
  57.7 0.7 dynamic_slice.37
  59.1 0.7 dynamic_slice.37
  60.6 0.7 dynamic_slice.37
  62.1 0.7 dynamic_slice.37
  63.6 0.7 dynamic_slice.37
  65.1 0.7 dynamic_slice.37
  66.6 0.7 dynamic_slice.37
  68.1 0.7 dynamic_slice.37
  69.5 0.7 dynamic_slice.37
  71.0 0.7 dynamic_slice.37
  72.5 0.7 dynamic_slice.37
  74.0 0.7 dynamic_slice.37
  75.5 0.7 dynamic_slice.37
  77.0 0.7 dynamic_slice.37
  78.5 0.7 dynamic_slice.37
  79.9 0.7 dynamic_slice.37
  81.4 0.7 dynamic_slice.37
  82.9 0.7 dynamic_slice.37
  84.4 0.7 dynamic_slice.37
  85.9 0.7 dynamic_slice.37
  87.4 0.7 dynamic_slice.37
  88.9 0.7 dynamic_slice.37
  90.3 0.7 dynamic_slice.37
  91.8 0.7 dynamic_slice.37
  93.3 0.7 dynamic_slice.37
  94.8 0.7 dynamic_slice.37
  96.3 0.7 dynamic_slice.37
  97.8 0.7 dynamic_slice.37
  99.3 0.7 dynamic_slice.37
  100.7 0.7 dynamic_slice.37
  142.3 22.0 %all-gather.3 = f32[16,4,1024]{2,1,0:T(4,128)S(1)} all-gather(f32[1,4,1024]{2,1,0:T(4,128)S(1)} %bitcast.45), channel_id=3, replica_groups=mesh['paths'=2,'tm'=16] {'tm'}, dimensions={0}, use_global_device_ids=true | all-gather | bytes 278528 | tf_op jit(solution)/shard_map/all_gather | solution.py:9
  164.4 17.6 %all-gather = f32[16384]{0:T(1024)S(1)} all-gather(f32[1024]{0:T(1024)S(1)} %get-tuple-element.124), channel_id=2, replica_groups=mesh['paths'=2,'tm'=16] {'tm'}, dimensions={0}, use_global_device_ids=true | all-gather | bytes 69632 | tf_op jit(solution)/shard_map/all_gather | solution.py:9
  182.9 19.7 %all-gather.4 = f32[16,1,4]{2,1,0:T(1,128)S(1)} all-gather(f32[1,1,4]{2,1,0:T(1,128)S(1)} %slice_bitcast_fusion), channel_id=1, replica_groups=mesh['paths'=2,'tm'=16] {'tm'}, dimensions={0}, use_global_device_ids=true | all-gather | bytes 272 | tf_op jit(solution)/shard_map/all_gather | solution.py:9
  203.1 17.5 %all-gather.5 = f32[16,4,128]{2,1,0:T(4,128)S(1)} all-gather(f32[1,4,128]{2,1,0:T(4,128)S(1)} %multiply_bitcast_fusion), channel_id=4, replica_groups=mesh['paths'=2,'tm'=16] {'tm'}, dimensions={0}, use_global_device_ids=true | all-gather | bytes 34816 | tf_op jit(solution)/shard_map/all_gather | solution.py:82
  (307 shorter events, 70.3 us)
Async XLA Ops:
  6.5 196.2 %copy-start = (bf16[1024,128]{1,0:T(8,128)(2,1)S(1)}, bf16[1024,128]{1,0:T(8,128)(2,1)}, u32[]{:S(2)}) copy-start(bf16[1024,128]{1,0:T(8,128)(2,1)} %param.18) | copy-start | bytes 786436
  6.5 38.2 %all-gather.8.cloned.1.call-start = ((), (), s32[]{:S(2)}) async-start(), calls=%async_computation | async-start | bytes 3145728 | tf_op jit(solution)/shard_map/all_gather | solution.py:34
  7.3 40.0 %copy-start.1 = (f32[64]{0:T(128)S(1)}, f32[64]{0:T(128)}, u32[]{:S(2)}) copy-start(f32[64]{0:T(128)} %param.17) | copy-start | bytes 772
Sparse Core Ops, SparseCore 0:
  8.9 35.8 all-gather.7
